TPU v7x, 256 devices: a whole 4x4x8 slice. The times are simulated.
256 devices in a mesh: rep: 8 (over x_lo, y), own: 32 (over z, x_hi, core).
Axes of the slice: x: 4 (x_hi: 2, x_lo: 2; x = x_hi * 2 + x_lo), y: 4, z: 8, core: 2. Of those that a mesh axis runs over, the one named last changes fastest.
Arguments:
- local_dense: bfloat16 [8, 1024, 187, 128], P('rep', 'own')
- owner_list: int32 [187], replicated, may hold values from 0 to 31, as said below
- anchor_slots: float32 [32, 1024, 12, 128], P('own', None, None, 'rep'), may hold values from -100 to 100
- moment_slots: float32 [32, 1024, 12, 128], P('own', None, None, 'rep'), may hold values from -3 to 3
- local_embed: bfloat16 [8, 26624, 1024], P('rep', 'own'), may hold values from -6 to 6
- anchor_embed: float32 [26624, 1024], P('own', 'rep'), may hold values from -6 to 6
- moment_embed: float32 [26624, 64], P('own'), may hold values from -3 to 3
- projection: bfloat16 [1024, 64], replicated, may hold values from -0.1875 to 0.1875
Outputs:
- dense_weights: bfloat16 [1024, 187, 128], P('own')
- anchor_slots_new: float32 [32, 1024, 12, 128], P('own', None, None, 'rep')
- moment_slots_new: float32 [32, 1024, 12, 128], P('own', None, None, 'rep')
- embed_weights: bfloat16 [26624, 1024], P('own')
- anchor_embed_new: float32 [26624, 1024], P('own', 'rep')
- moment_embed_new: float32 [26624, 64], P('own')
Inputs may be any that keep to these rules, and one draw needn't show every extreme that they name: `owner_list`: each owner holds at most 12 blocks, and some owner holds exactly 12.
All inputs are finite; a program needn't handle non-finite values.
Results may differ from a plain program's by a relative error of at most 0.015.
Values may be sent and summed in bfloat16 or wider, within the bound.
A program may use at most 128 MiB of HBM per device.

v0:
```python
import jax
import jax.numpy as jnp
from jax import lax
from jax.sharding import PartitionSpec as P

OUTER_MOMENTUM = 0.9
OUTER_RATE = 0.7
CLIP_RMS = 2.0
EPSILON = 1e-06


def slot_tables(owner_list, owners, capacity):
    unit_count = owner_list.shape[0]
    onehot = (owner_list[:, None] == jnp.arange(owners, dtype=jnp.int32)[None, :]).astype(jnp.int32)
    before = jnp.cumsum(onehot, axis=0) - onehot
    slot_rank = jnp.sum(before * onehot, axis=1)
    flat_index = owner_list * capacity + slot_rank
    matches = (
        jnp.arange(owners * capacity, dtype=jnp.int32)[:, None] == flat_index[None, :]
    ).astype(jnp.int32)
    slot_units = jnp.sum(matches * jnp.arange(unit_count, dtype=jnp.int32)[None, :], axis=1)
    live_slots = jnp.sum(matches, axis=1)
    return (flat_index, slot_units, live_slots)


def sum_over_groups(values):
    return lax.psum_scatter(
        values.astype(jnp.float32).astype(jnp.bfloat16), "rep", scatter_dimension=2, tiled=True
    ).astype(jnp.float32)


def on_device(
    local_dense,
    owner_list,
    anchor_slots,
    moment_slots,
    local_embed,
    anchor_embed,
    moment_embed,
    projection,
):
    owners = lax.axis_size("own")
    groups = lax.axis_size("rep")
    capacity = anchor_slots.shape[2]
    col_share = anchor_slots.shape[3]
    local_rows = local_dense.shape[1]
    pair_cols = local_dense.shape[3]
    model_width = local_rows * owners
    embed_cols_local = anchor_embed.shape[1]
    proj_cols = lax.dynamic_slice_in_dim(
        projection, lax.axis_index("rep") * embed_cols_local, embed_cols_local, 0
    ).astype(jnp.float32)
    partial_term = jnp.dot(anchor_embed, proj_cols, precision=lax.Precision.HIGHEST)
    partial_term = (
        partial_term
        - jnp.dot(local_embed[0], projection, preferred_element_type=jnp.float32) / groups
    )
    compressed = lax.psum(partial_term, "rep")
    moment_embed_new = OUTER_MOMENTUM * moment_embed + compressed
    anchor_embed_new = anchor_embed - OUTER_RATE * jnp.dot(
        compressed + OUTER_MOMENTUM * moment_embed_new, proj_cols.T, precision=lax.Precision.HIGHEST
    )
    embed_weights = lax.all_gather(anchor_embed_new.astype(jnp.bfloat16), "rep", axis=1, tiled=True)
    flat_index, slot_units, live_slots = slot_tables(owner_list, owners, capacity)
    stored = local_dense[0]
    packed = jnp.take(stored, slot_units, axis=1).reshape(local_rows, owners, capacity, pair_cols)
    arrived = lax.all_to_all(packed, "own", split_axis=1, concat_axis=0, tiled=True)
    owned_sum = sum_over_groups(arrived.reshape(model_width, capacity, pair_cols))
    owned_sum = owned_sum.reshape(1, model_width, capacity, col_share)
    change = anchor_slots - owned_sum / groups
    partial_value = jnp.sum(change * change, axis=(0, 1, 3))
    totals = lax.psum(partial_value, "rep")
    root_mean = jnp.sqrt(totals / (model_width * pair_cols) + EPSILON)
    factor = jnp.minimum(1.0, CLIP_RMS / root_mean).reshape(1, 1, capacity, 1)
    live_share = lax.dynamic_slice_in_dim(live_slots, lax.axis_index("own") * capacity, capacity, 0)
    live_share = live_share.astype(jnp.float32).reshape(1, 1, capacity, 1)
    clipped = change * factor
    moment_new = live_share * (OUTER_MOMENTUM * moment_slots + clipped)
    anchor_new = live_share * (anchor_slots - OUTER_RATE * (clipped + OUTER_MOMENTUM * moment_new))
    outgoing = anchor_new.astype(jnp.bfloat16).reshape(owners, local_rows, capacity, col_share)
    returned = lax.all_to_all(outgoing, "own", split_axis=0, concat_axis=2, tiled=True)
    placed = jnp.take(returned[0], flat_index, axis=1)
    dense_weights = lax.all_gather(placed, "rep", axis=2, tiled=True)
    return (
        dense_weights,
        anchor_new,
        moment_new,
        embed_weights,
        anchor_embed_new,
        moment_embed_new,
    )


def solution(mesh):
    placed = (
        P("rep", "own", None, None),
        P(),
        P("own", None, None, "rep"),
        P("own", None, None, "rep"),
        P("rep", "own", None),
        P("own", "rep"),
        P("own", None),
        P(),
    )
    return jax.shard_map(
        on_device,
        mesh=mesh,
        in_specs=placed,
        out_specs=(
            P("own", None, None),
            P("own", None, None, "rep"),
            P("own", None, None, "rep"),
            P("own", None),
            P("own", "rep"),
            P("own", None),
        ),
        check_vma=False,
    )
```

profile of v0, /device:TPU:24, one launch (start us, length us, event | category | flops | bytes accessed | tf_op | source)
XLA Modules:
  0.0 320.8 jit_solution(11099002583350050212)
XLA Ops:
  10.6 4.1 %gather_fusion = bf16[384,32,128]{2,1,0:T(8,128)(2,1)} fusion(bf16[32,187,128]{2,0,1:T(8,128)(2,1)} %bitcast.57, s32[1024]{0:T(1024)S(1)} %pad_clamp_fusion.1), kind=kCustom, calls=%fused_computation | custom fusion | bytes 6292992 | tf_op jit(solution)/shard_map/jit(_take)/gather | solution.py:66
  14.7 3.4 %broadcast_select_fusion = bf16[32,32,12,128]{3,0,2,1:T(8,128)(2,1)} fusion(bf16[32,32,12,128]{3,0,2,1:T(8,128)(2,1)} %bitcast.56, pred[32,12]{1,0:T(8,128)(4,1)S(1)} %compare_and_fusion), kind=kLoop, calls=%fused_computation.2 | loop fusion | flops 1572864 | bytes 6291840 | tf_op jit(solution)/shard_map/jit(_take)/select_n | solution.py:66
  18.1 11.6 %all-to-all-start = ((bf16[32,32,12,128]{3,0,2,1:T(8,128)(2,1)}), bf16[32,32,12,128]{3,0,2,1:T(8,128)(2,1)}, u32[]{:S(2)}, u32[]{:S(2)}) async-start(bf16[32,32,12,128]{3,0,2,1:T(8,128)(2,1)} %broadcast_select_fusion), calls=%async_computation | async-start | bytes 6291456 | tf_op jit(solution)/shard_map/all_to_all | solution.py:67
  31.8 72.1 %all-to-all-done = bf16[32,32,12,128]{3,0,2,1:T(8,128)(2,1)} async-done(((bf16[32,32,12,128]{3,0,2,1:T(8,128)(2,1)}), bf16[32,32,12,128]{3,0,2,1:T(8,128)(2,1)}, u32[]{:S(2)}, u32[]{:S(2)}) %all-to-all-start) | async-done | bytes 3145760 | tf_op jit(solution)/shard_map/all_to_all | solution.py:67
  103.9 4.3 %copy.74 = bf16[32,32,1,12,128]{4,1,0,3,2:T(8,128)(2,1)} copy(bf16[32,32,1,12,128]{4,1,3,0,2:T(8,128)(2,1)} %bitcast.5) | data formatting | bytes 6291456 | tf_op jit(solution)/shard_map/all_to_all | solution.py:67
  108.2 6.6 %copy.75 = bf16[1024,12,128]{0,1,2:T(8,128)(2,1)} copy(bf16[1024,12,128]{2,0,1:T(8,128)(2,1)} %bitcast.55) | data formatting | bytes 6291456 | tf_op jit(solution)/shard_map/reshape | solution.py:68
  116.7 2.4 fusion.23
  119.1 51.1 %reduce-scatter.2.cloned.1.call-done = bf16[1024,12,16]{0,1,2:T(8,128)(2,1)} async-done(((bf16[1024,12,128]{0,1,2:T(8,128)(2,1)}), bf16[1024,12,16]{0,1,2:T(8,128)(2,1)}) %reduce-scatter.2.cloned.1.call-update) | async-done | bytes 393232 | tf_op jit(solution)/shard_map/reduce_scatter | solution.py:27
  170.2 1.6 multiply_reduce_fusion
  171.9 16.6 %psum.14 = f32[12]{0:T(128)S(1)} all-reduce(f32[12]{0:T(128)S(1)} %multiply_reduce_fusion), channel_id=1, replica_groups=mesh['rep'=8,'own'=32] {'rep'}, use_global_device_ids=true, to_apply=%region_7.8 | all-reduce | flops 12 | bytes 96 | tf_op jit(solution)/shard_map/psum | solution.py:72
  188.5 3.7 %fusion.21 = (bf16[1,1024,12,16]{1,2,3,0:T(8,128)(2,1)}, f32[1,1024,12,16]{1,2,3,0:T(8,128)}, f32[1,1024,12,16]{1,2,3,0:T(8,128)}) fusion(f32[1,1024,12,16]{1,3,2,0:T(8,128)S(1)} %copy-done.6, f32[12]{0:T(128)S(1)} %multiply_minimum_fusion, bf16[1024,12,16]{0,1,2:T(8,128)(2,1)} %reduce-scatter.2.cloned.1.call-done, f32[1,1024,12,16]{1,3,2,0:T(8,128)S(1)} %copy-done.2, ...), kind=kLoop, calls=%fused_computation.51 | loop fusion | flops 2555904 | bytes 3932256 | tf_op jit(solution)/shard_map/convert_element_type | solution.py:80
  192.2 2.1 reshape.92
  194.3 2.2 copy.112
  196.5 3.7 %reshape.95 = bf16[32,2,3072]{2,1,0:T(2,128)(2,1)} reshape(bf16[32,12,16,32]{3,2,1,0:T(8,128)(2,1)} %bitcast.59) | data formatting | bytes 786432
  200.2 9.8 %all-to-all-start.1 = ((bf16[32,2,3072]{2,1,0:T(2,128)(2,1)}), bf16[32,2,3072]{2,1,0:T(2,128)(2,1)S(1)}, u32[]{:S(2)}, u32[]{:S(2)}) async-start(bf16[32,2,3072]{2,1,0:T(2,128)(2,1)} %reshape.95), calls=%async_computation.2 | async-start | bytes 786432 | tf_op jit(solution)/shard_map/all_to_all | solution.py:81
  210.3 15.1 %all-to-all-done.1 = bf16[32,2,3072]{2,1,0:T(2,128)(2,1)S(1)} async-done(((bf16[32,2,3072]{2,1,0:T(2,128)(2,1)}), bf16[32,2,3072]{2,1,0:T(2,128)(2,1)S(1)}, u32[]{:S(2)}, u32[]{:S(2)}) %all-to-all-start.1) | async-done | bytes 393248 | tf_op jit(solution)/shard_map/all_to_all | solution.py:81
  225.4 1.9 reshape.96
  227.3 2.2 gather_fusion.1
  229.5 1.1 select_bitcast_fusion
  230.7 2.6 copy.82
  233.2 1.3 copy.83
  234.6 72.4 %all-gather.3.cloned.1.call-done = bf16[32,187,128]{0,2,1:T(8,128)(2,1)} async-done(((bf16[32,187,16]{0,2,1:T(8,128)(2,1)}), bf16[32,187,128]{0,2,1:T(8,128)(2,1)}) %all-gather.3.cloned.1.call-update) | async-done | bytes 1531920 | tf_op jit(solution)/shard_map/all_gather | solution.py:83
  307.0 6.1 %copy.81 = bf16[32,187,128]{2,0,1:T(8,128)(2,1)} copy(bf16[32,187,128]{0,2,1:T(8,128)(2,1)} %all-gather.3.cloned.1.call-done) | data formatting | bytes 3063808
  313.1 1.2 copy.115
  (49 shorter events, 7.7 us)
Async XLA Ops:
  7.2 22.6 %copy-start = (bf16[1,832,1024]{2,1,0:T(8,128)(2,1)S(1)}, bf16[1,832,1024]{2,1,0:T(8,128)(2,1)}, u32[]{:S(2)}) copy-start(bf16[1,832,1024]{2,1,0:T(8,128)(2,1)} %param.12) | copy-start | bytes 5111812
  18.1 11.7 %copy-start.8 = (bf16[1024,64]{0,1:T(8,128)(2,1)S(1)}, bf16[1024,64]{0,1:T(8,128)(2,1)}, u32[]{:S(2)}) copy-start(bf16[1024,64]{0,1:T(8,128)(2,1)} %param.15) | copy-start | bytes 393220
  18.1 85.8 %all-to-all-start = ((bf16[32,32,12,128]{3,0,2,1:T(8,128)(2,1)}), bf16[32,32,12,128]{3,0,2,1:T(8,128)(2,1)}, u32[]{:S(2)}, u32[]{:S(2)}) async-start(bf16[32,32,12,128]{3,0,2,1:T(8,128)(2,1)} %broadcast_select_fusion), calls=%async_computation | async-start | bytes 6291456 | tf_op jit(solution)/shard_map/all_to_all | solution.py:67
  29.7 1.0 copy-start.3
  29.7 85.2 %all-reduce.3.cloned.1.call-start = ((), (), s32[]{:S(2)}) async-start(), calls=%async_computation.5 | async-start | bytes 458752 | tf_op jit(solution)/shard_map/psum | solution.py:58
  31.7 138.5 %reduce-scatter.2.cloned.1.call-start = ((), (), s32[]{:S(2)}) async-start(), calls=%async_computation.3 | async-start | bytes 4718592 | tf_op jit(solution)/shard_map/reduce_scatter | solution.py:27
  114.8 0.9 copy-start.7
  114.8 55.4 %copy-start.2 = (f32[1,1024,12,16]{1,3,2,0:T(8,128)S(1)}, f32[1,1024,12,16]{1,3,2,0:T(8,128)}, u32[]{:S(2)}) copy-start(f32[1,1024,12,16]{1,3,2,0:T(8,128)} %param.10) | copy-start | bytes 2359300
  114.8 115.8 %all-gather.5.cloned.1.call-start = ((), (), s32[]{:S(2)}) async-start(), calls=%async_computation.6 | async-start | bytes 1916928 | tf_op jit(solution)/shard_map/all_gather | solution.py:63
  116.7 2.4 copy-start.5
  119.1 69.4 %copy-start.6 = (f32[1,1024,12,16]{1,3,2,0:T(8,128)S(1)}, f32[1,1024,12,16]{1,3,2,0:T(8,128)}, u32[]{:S(2)}) copy-start(f32[1,1024,12,16]{1,3,2,0:T(8,128)} %param.11) | copy-start | bytes 2359300
  200.2 25.2 %all-to-all-start.1 = ((bf16[32,2,3072]{2,1,0:T(2,128)(2,1)}), bf16[32,2,3072]{2,1,0:T(2,128)(2,1)S(1)}, u32[]{:S(2)}, u32[]{:S(2)}) async-start(bf16[32,2,3072]{2,1,0:T(2,128)(2,1)} %reshape.95), calls=%async_computation.2 | async-start | bytes 786432 | tf_op jit(solution)/shard_map/all_to_all | solution.py:81
  210.0 96.9 %all-gather.3.cloned.1.call-start = ((), (), s32[]{:S(2)}) async-start(), calls=%async_computation.4 | async-start | bytes 6893568 | tf_op jit(solution)/shard_map/all_gather | solution.py:83
  229.4 3.8 %copy-start.1 = (f32[1,1024,12,16]{1,2,3,0:T(8,128)S(1)}, f32[1,1024,12,16]{1,2,3,0:T(8,128)}, u32[]{:S(2)}) copy-start(f32[1,1024,12,16]{1,2,3,0:T(8,128)} %get-tuple-element.48) | copy-start | bytes 2359300
  234.6 78.5 %copy-start.4 = (bf16[832,1024]{1,0:T(8,128)(2,1)S(1)}, bf16[832,1024]{1,0:T(8,128)(2,1)}, u32[]{:S(2)}) copy-start(bf16[832,1024]{1,0:T(8,128)(2,1)} %all-gather.5.cloned.1.call-done) | copy-start | bytes 5111812
Sparse Core Ops, SparseCore 0:
  33.7 79.4 all-reduce.2
  115.9 54.2 reduce-scatter.1
  172.6 47.1 all-gather.4
  230.7 76.1 all-gather.2
where the time goes:
time: 322 us; the launch traced here: 321 us
  waiting for transfers between devices  211 us (66%)
  local copies, waits for them, and re-layouts  39.6 us (12%)
  starting transfers between devices  21.7 us (7%)
  blocking collectives  16.6 us (5%)
  other arithmetic  14 us (4%)
  between operations  13.9 us (4%)
  matrix products  4.1 us (1%)
    all_gather x1, waiting for transfers between devices, on_device(): dense_weights = lax.all_gather(placed, 'rep', axis=2, tiled=True)  72.4 us
    all_to_all x1, waiting for transfers between devices, on_device(): lax.all_to_all(packed, 'own', split_axis=1, concat_axis=0, tiled=True)  72.1 us
    reduce_scatter x1, waiting for transfers between devices, sum_over_groups(): lax.psum_scatter(values.astype(jnp.float32).astype(jnp.bfloat16), 'rep',...  51.1 us
    unnamed x24, local copies, waits for them, and re-layouts  17.9 us
    psum x1, blocking collectives, on_device(): totals = lax.psum(partial_value, 'rep')  16.6 us
    all_to_all x1, waiting for transfers between devices, on_device(): lax.all_to_all(outgoing, 'own', split_axis=0, concat_axis=2, tiled=True)  15.1 us
    all_to_all x1, starting transfers between devices, on_device(): lax.all_to_all(packed, 'own', split_axis=1, concat_axis=0, tiled=True)  11.6 us
    all_to_all x1, starting transfers between devices, on_device(): lax.all_to_all(outgoing, 'own', split_axis=0, concat_axis=2, tiled=True)  9.81 us
  transfers between devices with their start and end apart: 6, of which 4 were waited for; matrix products, arithmetic and copies ran while one was open for 12% of the time, Pallas kernels for 0%

commit v1 on v0

v1 whole, which is shorter than its diff:
```python
import functools

import jax
import jax.numpy as jnp
from jax import lax
from jax.experimental import pallas as pl
from jax.experimental.pallas import tpu as pltpu
from jax.sharding import PartitionSpec as P

OUTER_MOMENTUM = 0.9
OUTER_RATE = 0.7
CLIP_RMS = 2.0
EPSILON = 1e-06
MESH = pl.DeviceIdType.MESH
F32 = jnp.float32
BF16 = jnp.bfloat16
HIGHEST = lax.Precision.HIGHEST


def iota(shape, axis):
    return lax.broadcasted_iota(jnp.int32, shape, axis)


def onehot(condition):
    return jnp.where(condition, 1.0, 0.0).astype(BF16)


def kernel(
    dims,
    dense_ref,
    owner_row_ref,
    owner_col_ref,
    anchor_ref,
    moment_ref,
    embed_ref,
    anchor_embed_ref,
    moment_embed_ref,
    projection_ref,
    dense_out,
    anchor_out,
    moment_out,
    embed_out,
    anchor_embed_out,
    moment_embed_out,
    stored,
    wide,
    share_send,
    share_recv,
    summed,
    slot_pick,
    unit_pick,
    to_rows,
    from_rows,
    out_send,
    out_recv,
    slots_f32,
    spread,
    change,
    squares_send,
    squares_recv,
    back_send,
    back_recv,
    column_send,
    column_recv,
    part_send,
    part_recv,
    part_sum,
    compressed,
    embed_send,
    share_sems,
    out_sems,
    squares_sems,
    back_sems,
    column_sems,
    part_sems,
    compressed_sems,
    embed_sems,
    local_sem,
):
    reps, owners, units, rows, cap, cols = dims
    lanes = reps * cols
    quads = rows // reps
    real = units * quads
    sent = share_send.shape[1]
    padded = summed.shape[0]
    block = quads * cap
    sources = owners * quads
    me_rep = lax.axis_index("rep")
    me_own = lax.axis_index("own")

    def rep_peer(step):
        return lax.rem(me_rep + step, reps)

    def rep_source(step):
        return lax.rem(me_rep + reps - step, reps)

    def own_peer(step):
        return lax.rem(me_own + step, owners)

    def own_source(step):
        return lax.rem(me_own + owners - step, owners)

    def rep_copy(src, dst, sems, step):
        return pltpu.make_async_remote_copy(
            src_ref=src,
            dst_ref=dst,
            send_sem=sems.at[0, step - 1],
            recv_sem=sems.at[1, step - 1],
            device_id=(rep_peer(step), me_own),
            device_id_type=MESH,
        )

    def own_copy(src, dst, sems, step):
        return pltpu.make_async_remote_copy(
            src_ref=src,
            dst_ref=dst,
            send_sem=sems.at[0, step - 1],
            recv_sem=sems.at[1, step - 1],
            device_id=(me_rep, own_peer(step)),
            device_id_type=MESH,
        )

    def loop(count, body):
        def run(step, carry):
            body(step)
            return carry

        lax.fori_loop(0, count, run, 0)

    def rep_loop(body):
        loop(reps - 1, lambda step: body(step + 1))

    def own_loop(body):
        loop(owners - 1, lambda step: body(step + 1))

    def aligned(start, size, by):
        return pl.ds(pl.multiple_of(start, by), size)

    barrier = pltpu.get_barrier_semaphore()
    rep_loop(
        lambda step: pl.semaphore_signal(
            barrier, inc=1, device_id=(rep_peer(step), me_own), device_id_type=MESH
        )
    )
    own_loop(
        lambda step: pl.semaphore_signal(
            barrier, inc=1, device_id=(me_rep, own_peer(step)), device_id_type=MESH
        )
    )

    anchor_embed = anchor_embed_ref[...]
    my_projection = projection_ref[:, aligned(me_rep * lanes, lanes, lanes)].astype(F32)
    last = (((1,), (1,)), ((), ()))
    part = lax.dot_general(my_projection, anchor_embed, last, precision=HIGHEST, preferred_element_type=F32)
    part_send[...] = part - lax.dot_general(
        projection_ref[...], embed_ref[...], last, preferred_element_type=F32
    ) / reps
    pl.semaphore_wait(barrier, reps - 1 + owners - 1)

    ranks = part_send.shape[0] // reps

    def part_copy(step):
        return rep_copy(
            part_send.at[aligned(rep_peer(step) * ranks, ranks, 8)], part_recv.at[step - 1], part_sems, step
        )

    rep_loop(lambda step: part_copy(step).start())

    row_count = dense_ref.shape[0]
    stored[pl.ds(0, row_count), :] = dense_ref[...].astype(F32)
    stored[pl.ds(row_count, padded * reps - row_count), :] = jnp.zeros(
        (padded * reps - row_count, lanes), F32
    )
    for group in range(reps):
        wide[:, group * lanes : (group + 1) * lanes] = stored[
            pl.ds(group, padded, stride=reps), :
        ].astype(BF16)

    def swap_pick(which):
        at = iota((reps * lanes, lanes), 0)
        lane = iota((reps * lanes, lanes), 1)
        return onehot(((at // lanes) * cols + at % cols == lane) & ((at // cols) % reps == which))

    def share_of(which):
        return jnp.dot(wide[...], swap_pick(which), preferred_element_type=F32)

    def share_copy(step):
        return rep_copy(share_send.at[step - 1], share_recv.at[step - 1], share_sems, step)

    def send_share(step):
        share_send[step - 1] = share_of(rep_peer(step))[:sent].astype(BF16)
        share_copy(step).start()

    rep_loop(send_share)
    summed_own = share_of(me_rep)[:sent]

    owner_row = owner_row_ref[...]
    owner_col = owner_col_ref[...]

    def targets(owner_at, owner_over, at_axis):
        shape = (padded, padded)
        at = iota(shape, at_axis)
        over = iota(shape, 1 - at_axis)
        before = (owner_at == owner_over) & (over < at) & (over % quads == at % quads)
        rank = jnp.sum(jnp.where(before, 1.0, 0.0), axis=1 - at_axis, keepdims=True).astype(jnp.int32)
        short = (1, padded) if at_axis == 1 else (padded, 1)
        quad = iota(short, at_axis)
        target = owner_at * block + (quad % quads) * cap + rank
        return jnp.where(quad < real, target, -1)

    row_targets = targets(owner_row, owner_col, 1)
    col_targets = targets(owner_col, owner_row, 0)
    slot_rows = slot_pick.shape[0]
    slot_pick[...] = onehot(iota((slot_rows, padded), 0) == row_targets)
    unit_pick[...] = onehot(iota((padded, slot_rows), 1) == col_targets)
    held = jnp.sum(
        jnp.where((owner_row == me_own) & (iota((1, padded), 1) < real), 1.0, 0.0), axis=1, keepdims=True
    )
    width = sources * reps
    at = iota((width, width), 0)
    to = iota((width, width), 1)
    to_rows[...] = onehot((at % sources) * reps + at // sources == to)
    from_rows[...] = onehot((at % reps) * sources + at // reps == to)

    my_ranks = aligned(me_rep * ranks, ranks, 8)
    rep_loop(lambda step: part_copy(step).wait_recv())
    total = part_send[my_ranks, :]
    for step in range(1, reps):
        total = total + part_recv[step - 1]
    part_sum[...] = total
    compressed[my_ranks, :] = total

    def compressed_copy(step, source):
        return rep_copy(part_sum, compressed.at[aligned(source * ranks, ranks, 8)], compressed_sems, step)

    rep_loop(lambda step: compressed_copy(step, me_rep).start())

    rep_loop(lambda step: share_copy(step).wait_recv())
    share_total = summed_own
    for step in range(1, reps):
        share_total = share_total + share_recv[step - 1].astype(F32)
    summed[pl.ds(0, sent), :] = share_total.astype(BF16)
    summed[pl.ds(sent, padded - sent), :] = jnp.zeros((padded - sent, lanes), BF16)
    packed = jnp.dot(slot_pick[...], summed[...], preferred_element_type=F32).astype(BF16)
    out_send[...] = packed

    def own_block(index):
        return aligned(index * block, block, 16)

    def out_copy(step, source):
        return own_copy(
            out_send.at[own_block(own_peer(step))], out_recv.at[own_block(source)], out_sems, step
        )

    own_loop(lambda step: out_copy(step, me_own).start())
    out_recv[own_block(me_own), :] = out_send[own_block(me_own), :]

    rep_loop(lambda step: compressed_copy(step, rep_source(step)).wait_recv())
    change_embed = compressed[...]
    moment_embed_new = OUTER_MOMENTUM * moment_embed_ref[...] + change_embed
    moment_embed_out[...] = moment_embed_new
    first = (((0,), (0,)), ((), ()))
    anchor_embed_new = anchor_embed_ref[...] - OUTER_RATE * lax.dot_general(
        change_embed + OUTER_MOMENTUM * moment_embed_new,
        my_projection,
        first,
        precision=HIGHEST,
        preferred_element_type=F32,
    )
    anchor_embed_out[...] = anchor_embed_new
    embed_send[...] = anchor_embed_new.astype(BF16)

    def embed_copy(step, source):
        return rep_copy(embed_send, embed_out.at[:, aligned(source * lanes, lanes, lanes)], embed_sems, step)

    half = reps // 2
    loop(half, lambda step: embed_copy(step + 1, me_rep).start())
    own_embed = pltpu.make_async_copy(
        embed_send, embed_out.at[:, aligned(me_rep * lanes, lanes, lanes)], local_sem
    )
    own_embed.start()

    own_loop(lambda step: out_copy(step, own_source(step)).wait_recv())
    slots_f32[...] = out_recv[...].astype(F32)
    for slot in range(cap):
        turned = slots_f32[pl.ds(slot, sources, stride=cap), :].T
        for group in range(reps):
            spread[slot * cols : (slot + 1) * cols, group * sources : (group + 1) * sources] = turned[
                group * cols : (group + 1) * cols
            ].astype(BF16)
    owned = jnp.dot(spread[...], to_rows[...], preferred_element_type=F32)
    change[...] = anchor_ref[...] - owned / reps
    squares_send[...] = jnp.zeros_like(squares_send)
    for slot in range(cap):
        one = change[slot * cols : (slot + 1) * cols, :]
        total = jnp.sum(jnp.sum(one * one, axis=0, keepdims=True), axis=1, keepdims=True)
        squares_send[slot : slot + 1, :] = jnp.broadcast_to(total, (1, squares_send.shape[1]))

    def squares_copy(step):
        return rep_copy(squares_send, squares_recv.at[step - 1], squares_sems, step)

    rep_loop(lambda step: squares_copy(step).start())
    loop(reps - 1 - half, lambda step: embed_copy(step + 1 + half, me_rep).start())
    rep_loop(lambda step: squares_copy(step).wait_recv())
    squares = squares_send[...]
    for step in range(1, reps):
        squares = squares + squares_recv[step - 1]
    root_mean = jnp.sqrt(squares / (owners * rows * lanes) + EPSILON)
    factors = jnp.minimum(1.0, CLIP_RMS / root_mean)
    for slot in range(cap):
        at = pl.ds(slot * cols, cols)
        live = jnp.where(held > slot * quads, 1.0, 0.0)
        clipped = change[at, :] * factors[slot : slot + 1, 0:1]
        moment_new = live * (OUTER_MOMENTUM * moment_ref[at, :] + clipped)
        anchor_new = live * (anchor_ref[at, :] - OUTER_RATE * (clipped + OUTER_MOMENTUM * moment_new))
        moment_out[at, :] = moment_new
        anchor_out[at, :] = anchor_new
        spread[at, :] = anchor_new.astype(BF16)
    regrouped = jnp.dot(spread[...], from_rows[...], preferred_element_type=F32)
    for slot in range(cap):
        turned = jnp.concatenate(
            [
                regrouped[slot * cols : (slot + 1) * cols, group * sources : (group + 1) * sources]
                for group in range(reps)
            ],
            axis=0,
        ).T
        slots_f32[pl.ds(slot, sources, stride=cap), :] = turned
    back_send[...] = slots_f32[...].astype(BF16)

    def back_copy(step, source):
        return own_copy(
            back_send.at[own_block(own_peer(step))], back_recv.at[own_block(source)], back_sems, step
        )

    own_loop(lambda step: back_copy(step, me_own).start())
    back_recv[own_block(me_own), :] = back_send[own_block(me_own), :]
    own_loop(lambda step: back_copy(step, own_source(step)).wait_recv())

    column_send[...] = jnp.dot(unit_pick[...], back_recv[...], preferred_element_type=F32)[:sent].astype(BF16)

    def column_copy(step, source):
        return rep_copy(column_send, column_recv.at[source], column_sems, step)

    rep_loop(lambda step: column_copy(step, me_rep).start())
    column_recv[me_rep] = column_send[...]
    rep_loop(lambda step: column_copy(step, rep_source(step)).wait_recv())
    gathered = jnp.concatenate([column_recv[group] for group in range(reps)], axis=1)
    for group in range(reps):
        stored[pl.ds(group, sent, stride=reps), :] = jnp.dot(
            gathered, swap_pick(group), preferred_element_type=F32
        )
    dense_out[...] = stored[pl.ds(0, row_count), :].astype(BF16)

    rep_loop(lambda step: embed_copy(step, rep_source(step)).wait_recv())
    own_embed.wait()
    rep_loop(lambda step: part_copy(step).wait_send())
    rep_loop(lambda step: share_copy(step).wait_send())
    rep_loop(lambda step: compressed_copy(step, me_rep).wait_send())
    rep_loop(lambda step: squares_copy(step).wait_send())
    rep_loop(lambda step: embed_copy(step, me_rep).wait_send())
    rep_loop(lambda step: column_copy(step, me_rep).wait_send())
    own_loop(lambda step: out_copy(step, me_own).wait_send())
    own_loop(lambda step: back_copy(step, me_own).wait_send())


def round_up(value, to):
    return -(-value // to) * to


def on_device(
    local_dense,
    owner_list,
    anchor_slots,
    moment_slots,
    local_embed,
    anchor_embed,
    moment_embed,
    projection,
):
    owners = lax.axis_size("own")
    reps = lax.axis_size("rep")
    _, rows, units, lanes = local_dense.shape
    _, width, cap, cols = anchor_slots.shape
    vocab, rank = moment_embed.shape
    features = projection.shape[0]
    quads = rows // reps
    real = units * quads
    sent = round_up(real, 16)
    padded = round_up(real, 128)
    block = quads * cap
    slot_rows = owners * block

    def turn_slots(slots):
        return jnp.transpose(slots[0], (1, 2, 0)).reshape(cap * cols, width)

    def unturn_slots(slots):
        return jnp.transpose(slots.reshape(cap, cols, width), (2, 0, 1))[None]

    owner_quads = jnp.pad(jnp.repeat(owner_list, quads), (0, padded - real))
    vmem = pl.BlockSpec(memory_space=pltpu.VMEM)
    rep_sems = pltpu.SemaphoreType.DMA((2, reps - 1))
    own_sems = pltpu.SemaphoreType.DMA((2, owners - 1))
    dense, anchor_new, moment_new, embed_weights, anchor_embed_new, moment_embed_new = pl.pallas_call(
        functools.partial(kernel, (reps, owners, units, rows, cap, cols)),
        out_shape=(
            jax.ShapeDtypeStruct((units * rows, lanes), BF16),
            jax.ShapeDtypeStruct((cap * cols, width), F32),
            jax.ShapeDtypeStruct((cap * cols, width), F32),
            jax.ShapeDtypeStruct((vocab, features), BF16),
            jax.ShapeDtypeStruct((vocab, lanes), F32),
            jax.ShapeDtypeStruct((rank, vocab), F32),
        ),
        in_specs=[vmem] * 9,
        out_specs=(vmem, vmem, vmem, pl.BlockSpec(memory_space=pl.ANY), vmem, vmem),
        scratch_shapes=[
            pltpu.VMEM((padded * reps, lanes), F32),
            pltpu.VMEM((padded, reps * lanes), BF16),
            pltpu.VMEM((reps - 1, sent, lanes), BF16),
            pltpu.VMEM((reps - 1, sent, lanes), BF16),
            pltpu.VMEM((padded, lanes), BF16),
            pltpu.VMEM((slot_rows, padded), BF16),
            pltpu.VMEM((padded, slot_rows), BF16),
            pltpu.VMEM((width, width), BF16),
            pltpu.VMEM((width, width), BF16),
            pltpu.VMEM((slot_rows, lanes), BF16),
            pltpu.VMEM((slot_rows, lanes), BF16),
            pltpu.VMEM((slot_rows, lanes), F32),
            pltpu.VMEM((cap * cols, width), BF16),
            pltpu.VMEM((cap * cols, width), F32),
            pltpu.VMEM((round_up(cap, 8), lanes), F32),
            pltpu.VMEM((reps - 1, round_up(cap, 8), lanes), F32),
            pltpu.VMEM((slot_rows, lanes), BF16),
            pltpu.VMEM((slot_rows, lanes), BF16),
            pltpu.VMEM((sent, lanes), BF16),
            pltpu.VMEM((reps, sent, lanes), BF16),
            pltpu.VMEM((rank, vocab), F32),
            pltpu.VMEM((reps - 1, rank // reps, vocab), F32),
            pltpu.VMEM((rank // reps, vocab), F32),
            pltpu.VMEM((rank, vocab), F32),
            pltpu.VMEM((vocab, lanes), BF16),
            rep_sems,
            own_sems,
            rep_sems,
            own_sems,
            rep_sems,
            rep_sems,
            rep_sems,
            rep_sems,
            pltpu.SemaphoreType.DMA,
        ],
        compiler_params=pltpu.CompilerParams(
            collective_id=0, has_side_effects=True, vmem_limit_bytes=62 * 1024 * 1024
        ),
        name="outer_step",
    )(
        jnp.transpose(local_dense[0], (1, 0, 2)).reshape(units * rows, lanes),
        owner_quads[None, :],
        owner_quads[:, None],
        turn_slots(anchor_slots),
        turn_slots(moment_slots),
        local_embed[0],
        anchor_embed,
        moment_embed.T,
        projection.T,
    )
    return (
        jnp.transpose(dense.reshape(units, rows, lanes), (1, 0, 2)),
        unturn_slots(anchor_new),
        unturn_slots(moment_new),
        embed_weights,
        anchor_embed_new,
        moment_embed_new.T,
    )


def solution(mesh):
    placed = (
        P("rep", "own", None, None),
        P(),
        P("own", None, None, "rep"),
        P("own", None, None, "rep"),
        P("rep", "own", None),
        P("own", "rep"),
        P("own", None),
        P(),
    )
    return jax.shard_map(
        on_device,
        mesh=mesh,
        in_specs=placed,
        out_specs=(
            P("own", None, None),
            P("own", None, None, "rep"),
            P("own", None, None, "rep"),
            P("own", None),
            P("own", "rep"),
            P("own", None),
        ),
        check_vma=False,
    )
```

time: 322 us -> 127 us (0.39)
  waiting for transfers between devices: 211 us -> 0 us
  Pallas kernels: 0 us -> 115 us
  local copies, waits for them, and re-layouts: 39.6 us -> 9.75 us
  starting transfers between devices: 21.7 us -> 0 us
  blocking collectives: 16.6 us -> 0 us
  other arithmetic: 14 us -> 0 us
  between operations: 13.9 us -> 0.69 us
  matrix products: 4.1 us -> 0 us
    pallas_call x0 -> x1, Pallas kernels: none -> 115 us  [on_device(): pl.pallas_call(functools.partial(kernel, (reps, owners, units, rows, cap,...]
    all_to_all x2 -> x0, waiting for transfers between devices: 87.2 us -> none  [the longest x1 72.1 us: on_device(): lax.all_to_all(packed, 'own', split_axis=1, concat_axis=0, tiled=True)]
    all_gather x2 -> x0, waiting for transfers between devices: 72.4 us -> none  [the longest x1 72.4 us: on_device(): dense_weights = lax.all_gather(placed, 'rep', axis=2, tiled=True)]
    reduce_scatter x1 -> x0, waiting for transfers between devices: 51.1 us -> none  [sum_over_groups(): lax.psum_scatter(values.astype(jnp.float32).astype(jnp.bfloat16), 'rep',...]
    all_to_all x2 -> x0, starting transfers between devices: 21.4 us -> none  [the longest x1 11.6 us: on_device(): lax.all_to_all(packed, 'own', split_axis=1, concat_axis=0, tiled=True)]
    psum x1 -> x0, blocking collectives: 16.6 us -> none  [on_device(): totals = lax.psum(partial_value, 'rep')]
    reshape x3 -> x1, local copies, waits for them, and re-layouts: 10.8 us -> 0.11 us  [on_device(): owner_quads = jnp.pad(jnp.repeat(owner_list, quads), (0, padded - real))]
    unnamed x24 -> x16, local copies, waits for them, and re-layouts: 17.9 us -> 7.39 us
  transfers between devices with their start and end apart: 6 -> 0, of which waited for: 4 -> 0; matrix products, arithmetic and copies ran while one was open for 12% -> 0% of each run, Pallas kernels for 0% -> 0%
where the time goes in v1:
time: 127 us; the launch traced here: 126 us
  Pallas kernels  115 us (91%)
  local copies, waits for them, and re-layouts  9.75 us (8%)
    pallas_call x1, Pallas kernels, on_device(): pl.pallas_call(functools.partial(kernel, (reps, owners, units, rows, cap,...  115 us
    unnamed x16, local copies, waits for them, and re-layouts  7.39 us

profile of v1, /device:TPU:24, one launch (start us, length us, event | category | flops | bytes accessed | tf_op | source)
XLA Modules:
  0.0 125.7 jit_solution(15812125758986810465)
XLA Ops:
  0.6 0.8 broadcast_in_dim.15
  1.4 0.1 reshape.34
  1.5 0.6 broadcast_in_dim.16.owner_row_ref
  2.1 0.9 broadcast_in_dim.20.owner_col_ref
  3.0 115.2 %outer_step.1 = (bf16[5984,128]{1,0:T(8,128)(2,1)}, f32[192,1024]{1,0:T(8,128)}, f32[192,1024]{1,0:T(8,128)}, bf16[832,1024]{1,0:T(8,128)(2,1)}, f32[832,128]{1,0:T(8,128)}, /*index=5*/f32[64,832]{1,0:T(8,128)}) custom-call(bf16[5984,128]{1,0:T(8,128)(2,1)} %bitcast.33, s32[1,768]{1,0:T(1,128)} %broadcast_in_dim.16.owner_row_ref, ...), custom_call_target="tpu_custom_call" | custom-call | tf_op jit(solution)/shard_map/outer_step/pallas_call | solution.py:404
  118.3 0.0 copy-start.2
  118.3 0.0 copy-start.1
  118.3 2.9 %copy.21 = bf16[32,187,128]{2,0,1:T(8,128)(2,1)} copy(bf16[32,187,128]{2,0,1:T(8,128)(2,1)} %bitcast.34) | data formatting | bytes 3063808
  121.2 0.0 copy-done.2
  121.2 0.0 copy-start
  121.2 0.9 copy.22
  122.1 0.0 copy-done.1
  122.1 0.9 copy.23
  123.0 0.0 copy-done
  123.0 0.0 copy-start.3
  123.0 0.0 copy-start.4
  123.0 1.2 copy.24
  124.2 0.1 copy-done.3
  124.2 0.8 copy.25
  125.0 0.0 copy-done.4
  125.0 0.7 copy.26
  (1 shorter events, 0.0 us)
Async XLA Ops:
  118.3 2.9 %copy-start.2 = (f32[192,1024]{1,0:T(8,128)S(1)}, f32[192,1024]{1,0:T(8,128)}, u32[]{:S(2)}) copy-start(f32[192,1024]{1,0:T(8,128)} %get-tuple-element.13) | copy-start | bytes 2359300
  118.3 3.8 %copy-start.1 = (f32[192,1024]{1,0:T(8,128)S(1)}, f32[192,1024]{1,0:T(8,128)}, u32[]{:S(2)}) copy-start(f32[192,1024]{1,0:T(8,128)} %get-tuple-element.14) | copy-start | bytes 2359300
  121.2 1.8 %copy-start = (bf16[832,1024]{1,0:T(8,128)(2,1)S(1)}, bf16[832,1024]{1,0:T(8,128)(2,1)}, u32[]{:S(2)}) copy-start(bf16[832,1024]{1,0:T(8,128)(2,1)} %get-tuple-element.27) | copy-start | bytes 5111812
  123.0 1.3 %copy-start.3 = (f32[832,128]{1,0:T(8,128)S(1)}, f32[832,128]{1,0:T(8,128)}, u32[]{:S(2)}) copy-start(f32[832,128]{1,0:T(8,128)} %get-tuple-element.28) | copy-start | bytes 1277956
  123.0 2.0 %copy-start.4 = (f32[64,832]{1,0:T(8,128)S(1)}, f32[64,832]{1,0:T(8,128)}, u32[]{:S(2)}) copy-start(f32[64,832]{1,0:T(8,128)} %get-tuple-element.17) | copy-start | bytes 638980

commit v2 on v1

v2 whole, which is shorter than its diff:
```python
import functools

import jax
import jax.numpy as jnp
from jax import lax
from jax.experimental import pallas as pl
from jax.experimental.pallas import tpu as pltpu
from jax.sharding import PartitionSpec as P

OUTER_MOMENTUM = 0.9
OUTER_RATE = 0.7
CLIP_RMS = 2.0
EPSILON = 1e-06
MESH = pl.DeviceIdType.MESH
F32 = jnp.float32
BF16 = jnp.bfloat16
HIGHEST = lax.Precision.HIGHEST


def iota(shape, axis):
    return lax.broadcasted_iota(jnp.int32, shape, axis)


def onehot(condition):
    return jnp.where(condition, 1.0, 0.0).astype(BF16)


def swap_matrix(reps, cols):
    lanes = reps * cols
    at = iota((reps * lanes, 1), 0)
    to = ((at // cols) % reps) * lanes + (at // lanes) * cols + at % cols
    return onehot(iota((reps * lanes, reps * lanes), 1) == to)


def kernel(
    dims,
    owner_ref,
    dense_hbm,
    embed_hbm,
    anchor_embed_hbm,
    projection_hbm,
    moment_embed_hbm,
    anchor_hbm,
    moment_hbm,
    column_out,
    embed_out,
    anchor_out,
    moment_out,
    anchor_embed_out,
    moment_embed_out,
    dense_ref,
    embed_ref,
    anchor_embed_ref,
    projection_ref,
    moment_embed_ref,
    anchor_ref,
    moment_ref,
    anchor_new_ref,
    moment_new_ref,
    anchor_embed_new_ref,
    moment_embed_new_ref,
    swap,
    stored,
    wide,
    share_send,
    share_recv,
    summed,
    slot_pick,
    unit_pick,
    to_rows,
    from_rows,
    out_send,
    out_recv,
    slots_f32,
    spread,
    change,
    squares_send,
    squares_recv,
    back_send,
    back_recv,
    column_send,
    part_send,
    part_recv,
    part_sum,
    compressed,
    embed_send,
    share_sems,
    out_sems,
    squares_sems,
    back_sems,
    part_sems,
    compressed_sems,
    column_sems,
    embed_sems,
    in_sems,
    local_sems,
):
    reps, owners, units, rows, cap, cols = dims
    lanes = reps * cols
    quads = rows // reps
    real = units * quads
    sent = share_send.shape[1]
    padded = summed.shape[0]
    block = quads * cap
    sources = owners * quads
    ring = reps // 2
    me_rep = lax.axis_index("rep")
    me_own = lax.axis_index("own")
    side = me_rep // ring
    place = lax.rem(me_rep, ring)

    def rep_at(flip, move):
        return lax.rem(side + flip, 2) * ring + lax.rem(place + move, ring)

    def rep_peer(step):
        return rep_at(step // ring, lax.rem(step, ring))

    def rep_source(step):
        return rep_at(step // ring, ring - lax.rem(step, ring))

    def own_peer(step):
        return lax.rem(me_own + step, owners)

    def own_source(step):
        return lax.rem(me_own + owners - step, owners)

    def send(src, dst, sems, index, device):
        return pltpu.make_async_remote_copy(
            src_ref=src,
            dst_ref=dst,
            send_sem=sems.at[0, index],
            recv_sem=sems.at[1, index],
            device_id=device,
            device_id_type=MESH,
        )

    def rep_copy(src, dst, sems, step):
        return send(src, dst, sems, step - 1, (rep_peer(step), me_own))

    def own_copy(src, dst, sems, step):
        return send(src, dst, sems, step - 1, (me_rep, own_peer(step)))

    def loop(count, body):
        def run(step, carry):
            body(step)
            return carry

        lax.fori_loop(0, count, run, 0)

    def rep_loop(body):
        loop(reps - 1, lambda step: body(step + 1))

    def own_loop(body):
        loop(owners - 1, lambda step: body(step + 1))

    def aligned(start, size, by):
        return pl.ds(pl.multiple_of(start, by), size)

    class Spread:
        def __init__(self, own, slots, sems):
            half = slots.shape[1] // 2 // 16 * 16
            first = pl.ds(0, half)
            second = pl.ds(half, slots.shape[1] - half)
            up, down, over = rep_at(0, 1), rep_at(0, ring - 1), rep_at(1, 0)
            over_up, over_down = rep_at(1, 1), rep_at(1, ring - 1)
            far, over_far = rep_at(0, 2), rep_at(1, 2)
            self.own_slot = slots.at[me_rep]
            self.own = own
            self.sems = sems
            self.sends = [
                (own, slots.at[me_rep], over),
                (own, slots.at[me_rep], up),
                (own, slots.at[me_rep], down),
                (slots.at[over], slots.at[over], up),
                (slots.at[over], slots.at[over], down),
                (slots.at[down, first], slots.at[down, first], up),
                (slots.at[up, second], slots.at[up, second], down),
                (slots.at[over_down, first], slots.at[over_down, first], up),
                (slots.at[over_up, second], slots.at[over_up, second], down),
            ]
            self.lands = [
                slots.at[over],
                slots.at[down],
                slots.at[up],
                slots.at[over_down],
                slots.at[over_up],
                slots.at[far, first],
                slots.at[far, second],
                slots.at[over_far, first],
                slots.at[over_far, second],
            ]

        def copy(self, index):
            src, dst, device = self.sends[index]
            return send(src, dst, self.sems, index, (device, me_own))

        def start(self, *indices):
            for index in indices:
                self.copy(index).start()

        def arrived(self, *indices):
            for index in indices:
                land = self.lands[index]
                send(land, land, self.sems, index, (rep_at(1, 0), me_own)).wait_recv()

        def finish(self):
            for index in range(len(self.sends)):
                self.copy(index).wait_send()

    def fetch(index, src, dst):
        return pltpu.make_async_copy(src, dst, in_sems.at[index])

    fetches = [
        fetch(0, dense_hbm, dense_ref),
        fetch(1, embed_hbm, embed_ref),
        fetch(2, anchor_embed_hbm, anchor_embed_ref),
        fetch(3, projection_hbm, projection_ref),
        fetch(4, moment_embed_hbm, moment_embed_ref),
        fetch(5, anchor_hbm, anchor_ref),
        fetch(6, moment_hbm, moment_ref),
    ]
    for one in fetches:
        one.start()

    barrier = pltpu.get_barrier_semaphore()
    rep_loop(
        lambda step: pl.semaphore_signal(
            barrier, inc=1, device_id=(rep_peer(step), me_own), device_id_type=MESH
        )
    )
    own_loop(
        lambda step: pl.semaphore_signal(
            barrier, inc=1, device_id=(me_rep, own_peer(step)), device_id_type=MESH
        )
    )

    swap[...] = swap_matrix(reps, cols)
    row_count = dense_ref.shape[0]
    fetches[0].wait()
    stored[pl.ds(0, row_count), :] = dense_ref[...].astype(F32)
    stored[pl.ds(row_count, padded * reps - row_count), :] = jnp.zeros(
        (padded * reps - row_count, lanes), F32
    )
    for group in range(reps):
        wide[:, group * lanes : (group + 1) * lanes] = stored[
            pl.ds(group, padded, stride=reps), :
        ].astype(BF16)

    def share_of(which):
        return jnp.dot(
            wide[...], swap[:, aligned(which * lanes, lanes, lanes)], preferred_element_type=F32
        )[:sent]

    def share_copy(step):
        return rep_copy(share_send.at[step - 1], share_recv.at[step - 1], share_sems, step)

    order = sorted(range(1, reps), key=lambda step: (step == ring, abs(step % ring - ring // 2)))
    for count, step in enumerate(order):
        share_send[step - 1] = share_of(rep_peer(step)).astype(BF16)
        if count == 0:
            pl.semaphore_wait(barrier, reps - 1 + owners - 1)
        share_copy(step).start()
    summed_own = share_of(me_rep)

    for one in fetches[1:]:
        one.wait()
    my_projection = projection_ref[:, aligned(me_rep * lanes, lanes, lanes)].astype(F32)
    last = (((1,), (1,)), ((), ()))
    part = lax.dot_general(
        my_projection, anchor_embed_ref[...], last, precision=HIGHEST, preferred_element_type=F32
    )
    part_send[...] = part - lax.dot_general(
        projection_ref[...], embed_ref[...], last, preferred_element_type=F32
    ) / reps
    ranks = part_send.shape[0] // reps

    def part_copy(step):
        return rep_copy(
            part_send.at[aligned(rep_peer(step) * ranks, ranks, 8)], part_recv.at[step - 1], part_sems, step
        )

    rep_loop(lambda step: part_copy(step).start())

    owners_of = owner_ref[...].astype(F32)
    expand = onehot(iota((units, padded), 0) == iota((units, padded), 1) // quads)
    owner_row = jnp.dot(
        jnp.broadcast_to(owners_of, (8, units)).astype(BF16), expand, preferred_element_type=F32
    )[0:1].astype(jnp.int32)
    owner_col = jnp.sum(
        jnp.where(iota((padded, units), 1) == iota((padded, units), 0) // quads, owners_of, 0.0),
        axis=1,
        keepdims=True,
    ).astype(jnp.int32)

    def targets(owner_at, owner_over, at_axis):
        shape = (padded, padded)
        at = iota(shape, at_axis)
        over = iota(shape, 1 - at_axis)
        before = (owner_at == owner_over) & (over < at) & (over % quads == at % quads)
        rank = jnp.sum(jnp.where(before, 1.0, 0.0), axis=1 - at_axis, keepdims=True).astype(jnp.int32)
        short = (1, padded) if at_axis == 1 else (padded, 1)
        quad = iota(short, at_axis)
        target = owner_at * block + (quad % quads) * cap + rank
        return jnp.where(quad < real, target, -1)

    row_targets = targets(owner_row, owner_col, 1)
    col_targets = targets(owner_col, owner_row, 0)
    slot_rows = slot_pick.shape[0]
    slot_pick[...] = onehot(iota((slot_rows, padded), 0) == row_targets)
    unit_pick[...] = onehot(iota((padded, slot_rows), 1) == col_targets)
    held = jnp.sum(
        jnp.where((owner_row == me_own) & (iota((1, padded), 1) < real), 1.0, 0.0), axis=1, keepdims=True
    )
    width = sources * reps
    at = iota((width, 1), 0)
    to = iota((width, width), 1)
    to_rows[...] = onehot((at % sources) * reps + at // sources == to)
    from_rows[...] = onehot((at % reps) * sources + at // reps == to)

    rep_loop(lambda step: share_copy(step).wait_recv())
    share_total = summed_own
    for step in range(1, reps):
        share_total = share_total + share_recv[step - 1].astype(F32)
    summed[pl.ds(0, sent), :] = share_total.astype(BF16)
    summed[pl.ds(sent, padded - sent), :] = jnp.zeros((padded - sent, lanes), BF16)
    out_send[...] = jnp.dot(slot_pick[...], summed[...], preferred_element_type=F32).astype(BF16)

    def own_block(index):
        return aligned(index * block, block, 16)

    def out_copy(step, source):
        return own_copy(
            out_send.at[own_block(own_peer(step))], out_recv.at[own_block(source)], out_sems, step
        )

    own_loop(lambda step: out_copy(step, me_own).start())
    out_recv[own_block(me_own), :] = out_send[own_block(me_own), :]

    my_ranks = aligned(me_rep * ranks, ranks, 8)
    rep_loop(lambda step: part_copy(step).wait_recv())
    total = part_send[my_ranks, :]
    for step in range(1, reps):
        total = total + part_recv[step - 1]
    part_sum[...] = total
    compressed[my_ranks, :] = total

    def compressed_copy(step, source):
        return rep_copy(part_sum, compressed.at[aligned(source * ranks, ranks, 8)], compressed_sems, step)

    rep_loop(lambda step: compressed_copy(step, me_rep).start())
    rep_loop(lambda step: compressed_copy(step, rep_source(step)).wait_recv())
    change_embed = compressed[...]
    moment_embed_new = OUTER_MOMENTUM * moment_embed_ref[...] + change_embed
    moment_embed_new_ref[...] = moment_embed_new
    first = (((0,), (0,)), ((), ()))
    anchor_embed_new = anchor_embed_ref[...] - OUTER_RATE * lax.dot_general(
        change_embed + OUTER_MOMENTUM * moment_embed_new,
        my_projection,
        first,
        precision=HIGHEST,
        preferred_element_type=F32,
    )
    anchor_embed_new_ref[...] = anchor_embed_new
    embed_send[...] = anchor_embed_new.astype(BF16)
    embed_spread = Spread(embed_send, embed_out, embed_sems)
    embed_spread.start(0, 1, 2)

    def store(index, src, dst):
        return pltpu.make_async_copy(src, dst, local_sems.at[index])

    stores = [
        store(0, embed_send, embed_spread.own_slot),
        store(1, anchor_embed_new_ref, anchor_embed_out),
        store(2, moment_embed_new_ref, moment_embed_out),
    ]
    for one in stores:
        one.start()

    own_loop(lambda step: out_copy(step, own_source(step)).wait_recv())
    slots_f32[...] = out_recv[...].astype(F32)
    for slot in range(cap):
        turned = slots_f32[pl.ds(slot, sources, stride=cap), :].T
        for group in range(reps):
            spread[slot * cols : (slot + 1) * cols, group * sources : (group + 1) * sources] = turned[
                group * cols : (group + 1) * cols
            ].astype(BF16)
    owned = jnp.dot(spread[...], to_rows[...], preferred_element_type=F32)
    change[...] = anchor_ref[...] - owned / reps
    squares_send[...] = jnp.zeros_like(squares_send)
    for slot in range(cap):
        one = change[slot * cols : (slot + 1) * cols, :]
        total = jnp.sum(jnp.sum(one * one, axis=0, keepdims=True), axis=1, keepdims=True)
        squares_send[slot : slot + 1, :] = jnp.broadcast_to(total, (1, squares_send.shape[1]))

    def squares_copy(step):
        return rep_copy(squares_send, squares_recv.at[step - 1], squares_sems, step)

    rep_loop(lambda step: squares_copy(step).start())
    embed_spread.arrived(0, 1, 2)
    embed_spread.start(3, 4, 5, 6)
    rep_loop(lambda step: squares_copy(step).wait_recv())
    squares = squares_send[...]
    for step in range(1, reps):
        squares = squares + squares_recv[step - 1]
    root_mean = jnp.sqrt(squares / (owners * rows * lanes) + EPSILON)
    factors = jnp.minimum(1.0, CLIP_RMS / root_mean)
    for slot in range(cap):
        at = pl.ds(slot * cols, cols)
        live = jnp.where(held > slot * quads, 1.0, 0.0)
        clipped = change[at, :] * factors[slot : slot + 1, 0:1]
        moment_new = live * (OUTER_MOMENTUM * moment_ref[at, :] + clipped)
        anchor_new = live * (anchor_ref[at, :] - OUTER_RATE * (clipped + OUTER_MOMENTUM * moment_new))
        moment_new_ref[at, :] = moment_new
        anchor_new_ref[at, :] = anchor_new
        spread[at, :] = anchor_new.astype(BF16)
    regrouped = jnp.dot(spread[...], from_rows[...], preferred_element_type=F32)
    for slot in range(cap):
        turned = jnp.concatenate(
            [
                regrouped[slot * cols : (slot + 1) * cols, group * sources : (group + 1) * sources]
                for group in range(reps)
            ],
            axis=0,
        ).T
        slots_f32[pl.ds(slot, sources, stride=cap), :] = turned
    back_send[...] = slots_f32[...].astype(BF16)

    def back_copy(step, source):
        return own_copy(
            back_send.at[own_block(own_peer(step))], back_recv.at[own_block(source)], back_sems, step
        )

    own_loop(lambda step: back_copy(step, me_own).start())
    back_recv[own_block(me_own), :] = back_send[own_block(me_own), :]
    late = [store(3, anchor_new_ref, anchor_out), store(4, moment_new_ref, moment_out)]
    for one in late:
        one.start()
    embed_spread.arrived(3, 4)
    embed_spread.start(7, 8)
    own_loop(lambda step: back_copy(step, own_source(step)).wait_recv())

    column_send[...] = jnp.dot(unit_pick[...], back_recv[...], preferred_element_type=F32)[:sent].astype(BF16)
    column_spread = Spread(column_send, column_out, column_sems)
    column_spread.start(0, 1, 2)
    late.append(store(5, column_send, column_spread.own_slot))
    late[-1].start()
    column_spread.arrived(0)
    column_spread.start(3, 4)
    column_spread.arrived(1)
    column_spread.start(5)
    column_spread.arrived(2)
    column_spread.start(6)
    column_spread.arrived(3)
    column_spread.start(7)
    column_spread.arrived(4)
    column_spread.start(8)

    for one in stores + late:
        one.wait()
    embed_spread.arrived(5, 6, 7, 8)
    embed_spread.finish()
    rep_loop(lambda step: part_copy(step).wait_send())
    rep_loop(lambda step: share_copy(step).wait_send())
    rep_loop(lambda step: compressed_copy(step, me_rep).wait_send())
    rep_loop(lambda step: squares_copy(step).wait_send())
    own_loop(lambda step: out_copy(step, me_own).wait_send())
    own_loop(lambda step: back_copy(step, me_own).wait_send())
    column_spread.arrived(5, 6, 7, 8)
    column_spread.finish()


def finish_kernel(
    cols,
    column_ref,
    embed_ref,
    anchor_ref,
    moment_ref,
    anchor_embed_ref,
    moment_embed_ref,
    dense_out,
    embed_out,
    anchor_out,
    moment_out,
    anchor_embed_out,
    moment_embed_out,
    swap,
    stored,
):
    reps, size, lanes = column_ref.shape

    @pl.when(pl.program_id(0) == 0)
    def _():
        swap[...] = swap_matrix(reps, cols)

    gathered = jnp.concatenate([column_ref[group] for group in range(reps)], axis=1)
    ordered = jnp.dot(gathered, swap[...], preferred_element_type=F32)
    for group in range(reps):
        stored[pl.ds(group, size, stride=reps), :] = ordered[:, group * lanes : (group + 1) * lanes]
    dense_out[...] = stored[...].astype(BF16)
    for group in range(reps):
        embed_out[:, group * lanes : (group + 1) * lanes] = embed_ref[group]
    anchor_out[...] = anchor_ref[...]
    moment_out[...] = moment_ref[...]
    anchor_embed_out[...] = anchor_embed_ref[...]
    moment_embed_out[...] = moment_embed_ref[...]


def round_up(value, to):
    return -(-value // to) * to


def on_device(
    local_dense,
    owner_list,
    anchor_slots,
    moment_slots,
    local_embed,
    anchor_embed,
    moment_embed,
    projection,
):
    owners = lax.axis_size("own")
    reps = lax.axis_size("rep")
    _, rows, units, lanes = local_dense.shape
    _, width, cap, cols = anchor_slots.shape
    vocab, rank = moment_embed.shape
    features = projection.shape[0]
    quads = rows // reps
    real = units * quads
    sent = round_up(real, 16)
    padded = round_up(real, 128)
    block = quads * cap
    slot_rows = owners * block
    slot_cols = cap * cols
    steps = 4

    def turn_slots(slots):
        return jnp.transpose(slots[0], (1, 2, 0)).reshape(slot_cols, width)

    def unturn_slots(slots):
        return jnp.transpose(slots.reshape(cap, cols, width), (2, 0, 1))[None]

    vmem = pl.BlockSpec(memory_space=pltpu.VMEM)
    anywhere = pl.BlockSpec(memory_space=pl.ANY)
    rep_sems = pltpu.SemaphoreType.DMA((2, reps - 1))
    own_sems = pltpu.SemaphoreType.DMA((2, owners - 1))
    spread_sems = pltpu.SemaphoreType.DMA((2, 9))
    slot_shape = pltpu.VMEM((slot_cols, width), F32)
    column, embed_new, *rest = pl.pallas_call(
        functools.partial(kernel, (reps, owners, units, rows, cap, cols)),
        out_shape=(
            jax.ShapeDtypeStruct((reps, sent, lanes), BF16),
            jax.ShapeDtypeStruct((reps, vocab, lanes), BF16),
            jax.ShapeDtypeStruct((slot_cols, width), F32),
            jax.ShapeDtypeStruct((slot_cols, width), F32),
            jax.ShapeDtypeStruct((vocab, lanes), F32),
            jax.ShapeDtypeStruct((rank, vocab), F32),
        ),
        in_specs=[vmem] + [anywhere] * 7,
        out_specs=(anywhere,) * 6,
        scratch_shapes=[
            pltpu.VMEM((units * rows, lanes), BF16),
            pltpu.VMEM((vocab, features), BF16),
            pltpu.VMEM((vocab, lanes), F32),
            pltpu.VMEM((rank, features), BF16),
            pltpu.VMEM((rank, vocab), F32),
            slot_shape,
            slot_shape,
            slot_shape,
            slot_shape,
            pltpu.VMEM((vocab, lanes), F32),
            pltpu.VMEM((rank, vocab), F32),
            pltpu.VMEM((reps * lanes, reps * lanes), BF16),
            pltpu.VMEM((padded * reps, lanes), F32),
            pltpu.VMEM((padded, reps * lanes), BF16),
            pltpu.VMEM((reps - 1, sent, lanes), BF16),
            pltpu.VMEM((reps - 1, sent, lanes), BF16),
            pltpu.VMEM((padded, lanes), BF16),
            pltpu.VMEM((slot_rows, padded), BF16),
            pltpu.VMEM((padded, slot_rows), BF16),
            pltpu.VMEM((width, width), BF16),
            pltpu.VMEM((width, width), BF16),
            pltpu.VMEM((slot_rows, lanes), BF16),
            pltpu.VMEM((slot_rows, lanes), BF16),
            pltpu.VMEM((slot_rows, lanes), F32),
            pltpu.VMEM((slot_cols, width), BF16),
            slot_shape,
            pltpu.VMEM((round_up(cap, 8), lanes), F32),
            pltpu.VMEM((reps - 1, round_up(cap, 8), lanes), F32),
            pltpu.VMEM((slot_rows, lanes), BF16),
            pltpu.VMEM((slot_rows, lanes), BF16),
            pltpu.VMEM((sent, lanes), BF16),
            pltpu.VMEM((rank, vocab), F32),
            pltpu.VMEM((reps - 1, rank // reps, vocab), F32),
            pltpu.VMEM((rank // reps, vocab), F32),
            pltpu.VMEM((rank, vocab), F32),
            pltpu.VMEM((vocab, lanes), BF16),
            rep_sems,
            own_sems,
            rep_sems,
            own_sems,
            rep_sems,
            rep_sems,
            spread_sems,
            spread_sems,
            pltpu.SemaphoreType.DMA((7,)),
            pltpu.SemaphoreType.DMA((6,)),
        ],
        compiler_params=pltpu.CompilerParams(
            collective_id=0, has_side_effects=True, vmem_limit_bytes=62 * 1024 * 1024
        ),
        name="outer_step",
    )(
        owner_list[None, :],
        jnp.transpose(local_dense[0], (1, 0, 2)).reshape(units * rows, lanes),
        local_embed[0],
        anchor_embed,
        projection.T,
        moment_embed.T,
        turn_slots(anchor_slots),
        turn_slots(moment_slots),
    )

    size = round_up(-(-sent // steps), 64)

    def part_of(shape):
        return pl.BlockSpec((shape[0] // steps,) + shape[1:], lambda step: (step, 0))

    plain = [part_of(one.shape) for one in rest]
    dense, embed_weights, anchor_new, moment_new, anchor_embed_new, moment_embed_new = pl.pallas_call(
        functools.partial(finish_kernel, cols),
        grid=(steps,),
        out_shape=(
            jax.ShapeDtypeStruct((units * rows, lanes), BF16),
            jax.ShapeDtypeStruct((vocab, features), BF16),
        )
        + tuple(jax.ShapeDtypeStruct(one.shape, F32) for one in rest),
        in_specs=[
            pl.BlockSpec((reps, size, lanes), lambda step: (0, step, 0)),
            pl.BlockSpec((reps, vocab // steps, lanes), lambda step: (0, step, 0)),
        ]
        + plain,
        out_specs=[
            pl.BlockSpec((size * reps, lanes), lambda step: (step, 0)),
            pl.BlockSpec((vocab // steps, features), lambda step: (step, 0)),
        ]
        + plain,
        scratch_shapes=[
            pltpu.VMEM((reps * lanes, reps * lanes), BF16),
            pltpu.VMEM((size * reps, lanes), F32),
        ],
        name="outer_step_finish",
    )(column, embed_new, *rest)
    return (
        jnp.transpose(dense.reshape(units, rows, lanes), (1, 0, 2)),
        unturn_slots(anchor_new),
        unturn_slots(moment_new),
        embed_weights,
        anchor_embed_new,
        moment_embed_new.T,
    )


def solution(mesh):
    placed = (
        P("rep", "own", None, None),
        P(),
        P("own", None, None, "rep"),
        P("own", None, None, "rep"),
        P("rep", "own", None),
        P("own", "rep"),
        P("own", None),
        P(),
    )
    return jax.shard_map(
        on_device,
        mesh=mesh,
        in_specs=placed,
        out_specs=(
            P("own", None, None),
            P("own", None, None, "rep"),
            P("own", None, None, "rep"),
            P("own", None),
            P("own", "rep"),
            P("own", None),
        ),
        check_vma=False,
    )
```

time: 127 us -> 91.5 us (0.72)
  Pallas kernels: 115 us -> 89.5 us
  local copies, waits for them, and re-layouts: 9.75 us -> 0 us
    pallas_call x1, Pallas kernels: 115 us -> 82.5 us  [on_device(): pl.pallas_call(functools.partial(kernel, (reps, owners, units, rows, cap,...]
    unnamed x16 -> x0, local copies, waits for them, and re-layouts: 7.39 us -> none
    pallas_call x0 -> x1, Pallas kernels: none -> 7.06 us  [on_device(): pl.pallas_call(functools.partial(finish_kernel, cols), grid=(steps,), out...]
    broadcast_in_dim x3 -> x0, local copies, waits for them, and re-layouts: 2.25 us -> none  [the longest x1 0.91 us: on_device(): owner_quads[:, None]]
where the time goes in v2:
time: 91.5 us; the launch traced here: 90.3 us
  Pallas kernels  89.5 us (98%)
    pallas_call x1, Pallas kernels, on_device(): pl.pallas_call(functools.partial(kernel, (reps, owners, units, rows, cap,...  82.5 us
    pallas_call x1, Pallas kernels, on_device(): pl.pallas_call(functools.partial(finish_kernel, cols), grid=(steps,), out...  7.06 us

profile of v2, /device:TPU:24, one launch (start us, length us, event | category | flops | bytes accessed | tf_op | source)
XLA Modules:
  0.0 90.3 jit_solution(2666005173820743250)
XLA Ops:
  0.6 82.5 %outer_step.1 = (bf16[8,752,128]{2,1,0:T(8,128)(2,1)}, bf16[8,832,128]{2,1,0:T(8,128)(2,1)}, f32[192,1024]{1,0:T(8,128)}, f32[192,1024]{1,0:T(8,128)}, f32[832,128]{1,0:T(8,128)}, /*index=5*/f32[64,832]{1,0:T(8,128)}) custom-call(s32[1,187]{1,0:T(1,128)} %bitcast.39, bf16[5984,128]{1,0:T(8,128)(2,1)} %bitcast.34, bf16[832,1024]{1,0:T(8,128)(2,1)} %bitcast.33, ...), custom_call_target="tpu_custom_call" | custom-call | tf_op jit(solution)/shard_map/outer_step/pallas_call | solution.py:549
  83.1 7.1 %outer_step_finish.1 = (bf16[5984,128]{1,0:T(8,128)(2,1)}, bf16[832,1024]{1,0:T(8,128)(2,1)}, f32[192,1024]{1,0:T(8,128)}, f32[192,1024]{1,0:T(8,128)}, f32[832,128]{1,0:T(8,128)}, /*index=5*/f32[64,832]{1,0:T(8,128)}) custom-call(bf16[8,752,128]{2,1,0:T(8,128)(2,1)} %get-tuple-element.18.column_ref, bf16[8,832,128]{2,1,0:T(8,128)(2,1)} %get-tuple-element.19.embed_ref, ...), custom_call_target="tpu_custom_call" | custom-call | tf_op jit(solution)/shard_map/outer_step_finish/pallas_call | solution.py:630

commit v3 on v2

--- a/solution.py
+++ b/solution.py
@@ -63,7 +63,12 @@
     stored,
     wide,
     share_send,
-    share_recv,
+    far_recv,
+    near_recv,
+    joined_send,
+    joined_recv,
+    cross_send,
+    cross_recv,
     summed,
     slot_pick,
     unit_pick,
@@ -99,7 +104,7 @@
     lanes = reps * cols
     quads = rows // reps
     real = units * quads
-    sent = share_send.shape[1]
+    sent = share_send.shape[2]
     padded = summed.shape[0]
     block = quads * cap
     sources = owners * quads
@@ -251,16 +256,70 @@
             wide[...], swap[:, aligned(which * lanes, lanes, lanes)], preferred_element_type=F32
         )[:sent]
 
-    def share_copy(step):
-        return rep_copy(share_send.at[step - 1], share_recv.at[step - 1], share_sems, step)
-
-    order = sorted(range(1, reps), key=lambda step: (step == ring, abs(step % ring - ring // 2)))
-    for count, step in enumerate(order):
-        share_send[step - 1] = share_of(rep_peer(step)).astype(BF16)
-        if count == 0:
-            pl.semaphore_wait(barrier, reps - 1 + owners - 1)
-        share_copy(step).start()
-    summed_own = share_of(me_rep)
+    up, down = 1, ring - 1
+    cut = sent // 2 // 16 * 16
+    upper, lower = pl.ds(0, cut), pl.ds(cut, sent - cut)
+    FAR, UP, DOWN, SELF = range(4)
+
+    def hop(turn, index):
+        src, dst, part, move = (
+            (share_send.at[turn, FAR], far_recv, upper, up),
+            (share_send.at[turn, FAR], far_recv, lower, down),
+            (share_send.at[turn, UP], near_recv, lower, up),
+            (share_send.at[turn, DOWN], near_recv, upper, down),
+            (joined_send.at[turn], joined_recv, upper, up),
+            (joined_send.at[turn], joined_recv, lower, down),
+        )[index]
+        return send(
+            src.at[part], dst.at[turn, part], share_sems, turn * 6 + index, (rep_at(0, move), me_own)
+        )
+
+    def cross():
+        return send(cross_send, cross_recv, share_sems, 12, (rep_at(1, 0), me_own))
+
+    def pack(turn, kind):
+        move = (2, up, down, 0)[kind]
+        share_send[turn, kind] = share_of(rep_at(1 - turn, move)).astype(BF16)
+
+    def join(turn, index, part, kind):
+        hop(turn, index).wait_recv()
+        joined_send[turn, part, :] = (
+            far_recv[turn, part, :].astype(F32) + share_send[turn, kind, part, :].astype(F32)
+        ).astype(BF16)
+        hop(turn, index + 4).start()
+
+    def ring_total(turn):
+        for index in range(2, 6):
+            hop(turn, index).wait_recv()
+        return (
+            share_send[turn, SELF].astype(F32)
+            + near_recv[turn].astype(F32)
+            + joined_recv[turn].astype(F32)
+        )
+
+    pack(0, FAR)
+    pl.semaphore_wait(barrier, reps - 1 + owners - 1)
+    hop(0, 0).start()
+    hop(0, 1).start()
+    pack(0, UP)
+    hop(0, 2).start()
+    pack(0, DOWN)
+    hop(0, 3).start()
+    pack(1, FAR)
+    hop(1, 0).start()
+    hop(1, 1).start()
+    pack(0, SELF)
+    join(0, 0, upper, UP)
+    join(0, 1, lower, DOWN)
+    pack(1, UP)
+    hop(1, 2).start()
+    pack(1, DOWN)
+    hop(1, 3).start()
+    pack(1, SELF)
+    join(1, 0, upper, UP)
+    join(1, 1, lower, DOWN)
+    cross_send[...] = ring_total(0).astype(BF16)
+    cross().start()
 
     for one in fetches[1:]:
         one.wait()
@@ -317,10 +376,9 @@
     to_rows[...] = onehot((at % sources) * reps + at // sources == to)
     from_rows[...] = onehot((at % reps) * sources + at // reps == to)
 
-    rep_loop(lambda step: share_copy(step).wait_recv())
-    share_total = summed_own
-    for step in range(1, reps):
-        share_total = share_total + share_recv[step - 1].astype(F32)
+    share_total = ring_total(1)
+    cross().wait_recv()
+    share_total = share_total + cross_recv[...].astype(F32)
     summed[pl.ds(0, sent), :] = share_total.astype(BF16)
     summed[pl.ds(sent, padded - sent), :] = jnp.zeros((padded - sent, lanes), BF16)
     out_send[...] = jnp.dot(slot_pick[...], summed[...], preferred_element_type=F32).astype(BF16)
@@ -460,7 +518,10 @@
     embed_spread.arrived(5, 6, 7, 8)
     embed_spread.finish()
     rep_loop(lambda step: part_copy(step).wait_send())
-    rep_loop(lambda step: share_copy(step).wait_send())
+    for index in range(6):
+        hop(0, index).wait_send()
+        hop(1, index).wait_send()
+    cross().wait_send()
     rep_loop(lambda step: compressed_copy(step, me_rep).wait_send())
     rep_loop(lambda step: squares_copy(step).wait_send())
     own_loop(lambda step: out_copy(step, me_own).wait_send())
@@ -532,7 +593,7 @@
     block = quads * cap
     slot_rows = owners * block
     slot_cols = cap * cols
-    steps = 4
+    steps = 2
 
     def turn_slots(slots):
         return jnp.transpose(slots[0], (1, 2, 0)).reshape(slot_cols, width)
@@ -546,6 +607,7 @@
     own_sems = pltpu.SemaphoreType.DMA((2, owners - 1))
     spread_sems = pltpu.SemaphoreType.DMA((2, 9))
     slot_shape = pltpu.VMEM((slot_cols, width), F32)
+    ring_shape = pltpu.VMEM((2, sent, lanes), BF16)
     column, embed_new, *rest = pl.pallas_call(
         functools.partial(kernel, (reps, owners, units, rows, cap, cols)),
         out_shape=(
@@ -573,8 +635,13 @@
             pltpu.VMEM((reps * lanes, reps * lanes), BF16),
             pltpu.VMEM((padded * reps, lanes), F32),
             pltpu.VMEM((padded, reps * lanes), BF16),
-            pltpu.VMEM((reps - 1, sent, lanes), BF16),
-            pltpu.VMEM((reps - 1, sent, lanes), BF16),
+            pltpu.VMEM((2, 4, sent, lanes), BF16),
+            ring_shape,
+            ring_shape,
+            ring_shape,
+            ring_shape,
+            pltpu.VMEM((sent, lanes), BF16),
+            pltpu.VMEM((sent, lanes), BF16),
             pltpu.VMEM((padded, lanes), BF16),
             pltpu.VMEM((slot_rows, padded), BF16),
             pltpu.VMEM((padded, slot_rows), BF16),
@@ -595,7 +662,7 @@
             pltpu.VMEM((rank // reps, vocab), F32),
             pltpu.VMEM((rank, vocab), F32),
             pltpu.VMEM((vocab, lanes), BF16),
-            rep_sems,
+            pltpu.SemaphoreType.DMA((2, 13)),
             own_sems,
             rep_sems,
             own_sems,

time: 91.5 us -> 87 us (0.951)
  Pallas kernels: 89.5 us -> 85.6 us
    pallas_call x1, Pallas kernels: 82.5 us -> 79.1 us  [on_device(): pl.pallas_call(functools.partial(kernel, (reps, owners, units, rows, cap,...]
where the time goes in v3:
time: 87 us; the launch traced here: 86.4 us
  Pallas kernels  85.6 us (98%)
    pallas_call x1, Pallas kernels, on_device(): pl.pallas_call(functools.partial(kernel, (reps, owners, units, rows, cap,...  79.1 us
    pallas_call x1, Pallas kernels, on_device(): pl.pallas_call(functools.partial(finish_kernel, cols), grid=(steps,), out...  6.52 us

profile of v3, /device:TPU:24, one launch (start us, length us, event | category | flops | bytes accessed | tf_op | source)
XLA Modules:
  0.0 86.4 jit_solution(15146007336449311069)
XLA Ops:
  0.6 79.1 %outer_step.1 = (bf16[8,752,128]{2,1,0:T(8,128)(2,1)}, bf16[8,832,128]{2,1,0:T(8,128)(2,1)}, f32[192,1024]{1,0:T(8,128)}, f32[192,1024]{1,0:T(8,128)}, f32[832,128]{1,0:T(8,128)}, /*index=5*/f32[64,832]{1,0:T(8,128)}) custom-call(s32[1,187]{1,0:T(1,128)} %bitcast.39, bf16[5984,128]{1,0:T(8,128)(2,1)} %bitcast.34, bf16[832,1024]{1,0:T(8,128)(2,1)} %bitcast.33, ...), custom_call_target="tpu_custom_call" | custom-call | tf_op jit(solution)/shard_map/outer_step/pallas_call | solution.py:611
  79.7 6.5 %outer_step_finish.1 = (bf16[5984,128]{1,0:T(8,128)(2,1)}, bf16[832,1024]{1,0:T(8,128)(2,1)}, f32[192,1024]{1,0:T(8,128)}, f32[192,1024]{1,0:T(8,128)}, f32[832,128]{1,0:T(8,128)}, /*index=5*/f32[64,832]{1,0:T(8,128)}) custom-call(bf16[8,752,128]{2,1,0:T(8,128)(2,1)} %get-tuple-element.18.column_ref, bf16[8,832,128]{2,1,0:T(8,128)(2,1)} %get-tuple-element.19.embed_ref, ...), custom_call_target="tpu_custom_call" | custom-call | tf_op jit(solution)/shard_map/outer_step_finish/pallas_call | solution.py:697

commit v4 on v3

--- a/solution.py
+++ b/solution.py
@@ -174,25 +174,33 @@
             self.sems = sems
             self.sends = [
                 (own, slots.at[me_rep], over),
-                (own, slots.at[me_rep], up),
-                (own, slots.at[me_rep], down),
-                (slots.at[over], slots.at[over], up),
-                (slots.at[over], slots.at[over], down),
+                (own.at[first], slots.at[me_rep, first], up),
+                (own.at[second], slots.at[me_rep, second], down),
+                (slots.at[over, first], slots.at[over, first], up),
+                (slots.at[over, second], slots.at[over, second], down),
                 (slots.at[down, first], slots.at[down, first], up),
                 (slots.at[up, second], slots.at[up, second], down),
                 (slots.at[over_down, first], slots.at[over_down, first], up),
                 (slots.at[over_up, second], slots.at[over_up, second], down),
+                (own.at[second], slots.at[me_rep, second], up),
+                (own.at[first], slots.at[me_rep, first], down),
+                (slots.at[over, second], slots.at[over, second], up),
+                (slots.at[over, first], slots.at[over, first], down),
             ]
             self.lands = [
                 slots.at[over],
-                slots.at[down],
-                slots.at[up],
-                slots.at[over_down],
-                slots.at[over_up],
+                slots.at[down, first],
+                slots.at[up, second],
+                slots.at[over_down, first],
+                slots.at[over_up, second],
                 slots.at[far, first],
                 slots.at[far, second],
                 slots.at[over_far, first],
                 slots.at[over_far, second],
+                slots.at[down, second],
+                slots.at[up, first],
+                slots.at[over_down, second],
+                slots.at[over_up, first],
             ]
 
         def copy(self, index):
@@ -421,7 +429,7 @@
     anchor_embed_new_ref[...] = anchor_embed_new
     embed_send[...] = anchor_embed_new.astype(BF16)
     embed_spread = Spread(embed_send, embed_out, embed_sems)
-    embed_spread.start(0, 1, 2)
+    embed_spread.start(0, 1, 2, 9, 10)
 
     def store(index, src, dst):
         return pltpu.make_async_copy(src, dst, local_sems.at[index])
@@ -455,7 +463,7 @@
 
     rep_loop(lambda step: squares_copy(step).start())
     embed_spread.arrived(0, 1, 2)
-    embed_spread.start(3, 4, 5, 6)
+    embed_spread.start(3, 4, 11, 12, 5, 6)
     rep_loop(lambda step: squares_copy(step).wait_recv())
     squares = squares_send[...]
     for step in range(1, reps):
@@ -499,15 +507,15 @@
 
     column_send[...] = jnp.dot(unit_pick[...], back_recv[...], preferred_element_type=F32)[:sent].astype(BF16)
     column_spread = Spread(column_send, column_out, column_sems)
-    column_spread.start(0, 1, 2)
+    column_spread.start(0, 1, 2, 9, 10)
     late.append(store(5, column_send, column_spread.own_slot))
     late[-1].start()
-    column_spread.arrived(0)
-    column_spread.start(3, 4)
     column_spread.arrived(1)
     column_spread.start(5)
     column_spread.arrived(2)
     column_spread.start(6)
+    column_spread.arrived(0)
+    column_spread.start(3, 4, 11, 12)
     column_spread.arrived(3)
     column_spread.start(7)
     column_spread.arrived(4)
@@ -515,7 +523,7 @@
 
     for one in stores + late:
         one.wait()
-    embed_spread.arrived(5, 6, 7, 8)
+    embed_spread.arrived(*range(5, 13))
     embed_spread.finish()
     rep_loop(lambda step: part_copy(step).wait_send())
     for index in range(6):
@@ -526,7 +534,7 @@
     rep_loop(lambda step: squares_copy(step).wait_send())
     own_loop(lambda step: out_copy(step, me_own).wait_send())
     own_loop(lambda step: back_copy(step, me_own).wait_send())
-    column_spread.arrived(5, 6, 7, 8)
+    column_spread.arrived(*range(5, 13))
     column_spread.finish()
 
 
@@ -605,7 +613,7 @@
     anywhere = pl.BlockSpec(memory_space=pl.ANY)
     rep_sems = pltpu.SemaphoreType.DMA((2, reps - 1))
     own_sems = pltpu.SemaphoreType.DMA((2, owners - 1))
-    spread_sems = pltpu.SemaphoreType.DMA((2, 9))
+    spread_sems = pltpu.SemaphoreType.DMA((2, 13))
     slot_shape = pltpu.VMEM((slot_cols, width), F32)
     ring_shape = pltpu.VMEM((2, sent, lanes), BF16)
     column, embed_new, *rest = pl.pallas_call(

time: 87 us -> 85.6 us (0.984)
  Pallas kernels: 85.6 us -> 84.4 us
    pallas_call x1, Pallas kernels: 79.1 us -> 77.9 us  [on_device(): pl.pallas_call(functools.partial(kernel, (reps, owners, units, rows, cap,...]
where the time goes in v4:
time: 85.6 us; the launch traced here: 85.2 us
  Pallas kernels  84.4 us (99%)
    pallas_call x1, Pallas kernels, on_device(): pl.pallas_call(functools.partial(kernel, (reps, owners, units, rows, cap,...  77.9 us
    pallas_call x1, Pallas kernels, on_device(): pl.pallas_call(functools.partial(finish_kernel, cols), grid=(steps,), out...  6.52 us

profile of v4, /device:TPU:24, one launch (start us, length us, event | category | flops | bytes accessed | tf_op | source)
XLA Modules:
  0.0 85.2 jit_solution(140401515896567325)
XLA Ops:
  0.6 77.9 %outer_step.1 = (bf16[8,752,128]{2,1,0:T(8,128)(2,1)}, bf16[8,832,128]{2,1,0:T(8,128)(2,1)}, f32[192,1024]{1,0:T(8,128)}, f32[192,1024]{1,0:T(8,128)}, f32[832,128]{1,0:T(8,128)}, /*index=5*/f32[64,832]{1,0:T(8,128)}) custom-call(s32[1,187]{1,0:T(1,128)} %bitcast.39, bf16[5984,128]{1,0:T(8,128)(2,1)} %bitcast.34, bf16[832,1024]{1,0:T(8,128)(2,1)} %bitcast.33, ...), custom_call_target="tpu_custom_call" | custom-call | tf_op jit(solution)/shard_map/outer_step/pallas_call | solution.py:619
  78.5 6.5 %outer_step_finish.1 = (bf16[5984,128]{1,0:T(8,128)(2,1)}, bf16[832,1024]{1,0:T(8,128)(2,1)}, f32[192,1024]{1,0:T(8,128)}, f32[192,1024]{1,0:T(8,128)}, f32[832,128]{1,0:T(8,128)}, /*index=5*/f32[64,832]{1,0:T(8,128)}) custom-call(bf16[8,752,128]{2,1,0:T(8,128)(2,1)} %get-tuple-element.18.column_ref, bf16[8,832,128]{2,1,0:T(8,128)(2,1)} %get-tuple-element.19.embed_ref, ...), custom_call_target="tpu_custom_call" | custom-call | tf_op jit(solution)/shard_map/outer_step_finish/pallas_call | solution.py:705
